TPU v7x, 32 devices: a whole 2x2x4 slice. The times are simulated.
32 devices in a mesh: cache: 8 (over z, x), owner: 4 (over y, core).
Axes of the slice: x: 2, y: 2, z: 4, core: 2. Of those that a mesh axis runs over, the one named last changes fastest.
Arguments:
- cache: bfloat16 [32, 4, 128, 256], P('cache'), may hold values from -2.5 to 2.5
- backing: bfloat16 [32, 32, 128, 256], P('cache', 'owner'), may hold values from -2.5 to 2.5
- resident: int32 [32, 4], P('cache'), may hold values from 0 to 31, as said below
- promote: int32 [32, 2], P('cache'), may hold values from 0 to 31, as said below
- victim: int32 [32, 2], P('cache'), may hold values from 0 to 3, as said below
- lookups: int32 [2, 4096, 32, 8], P(None, 'owner', 'cache'), may hold values from 0 to 511
- route: int32 [2, 4, 1024], P(None, 'owner'), may hold values from 0 to 1023, each once within a row
- dcn_down: bfloat16 [8192, 128], P('cache'), may hold values from -0.0625 to 0.0625
- dcn_up: bfloat16 [128, 8192], P(None, 'cache'), may hold values from -0.5 to 0.5
- dcn_bias: float32 [8192], replicated, may hold values from -5 to 5
- mlp_in: bfloat16 [8192, 1024], P('cache'), may hold values from -0.0625 to 0.0625
- mlp_bias: float32 [1024], replicated, may hold values from -3 to 3
- mlp_out: float32 [1024], replicated, may hold values from -0.1875 to 0.1875
- out_bias: float32 [1], replicated, may hold values from -4 to 4
Outputs:
- scores: float32 [2, 4, 1024], P(None, 'owner', 'cache')
- new_cache: bfloat16 [32, 4, 128, 256], P('cache')
- new_backing: bfloat16 [32, 32, 128, 256], P('cache', 'owner')
Inputs may be any that keep to these rules, and one draw needn't show every extreme that they name: `resident`: for each feature, 4 distinct backing blocks. `promote`: for each feature, 2 distinct backing blocks, none of them in that feature's resident; block k belongs to owner k // 8. `victim`: for each feature, 2 distinct slots. `route`: each batch and owner group holds every request index once.
All inputs are finite; a program needn't handle non-finite values.
Results may differ from a plain program's by a relative error of at most 0.004.
Values may be sent and summed in bfloat16 or wider, within the bound.
A program may use at most 128 MiB of HBM per device.

v0:
```python
import jax
import jax.numpy as jnp
from jax import lax
from jax.sharding import PartitionSpec as P


def take_rows(table, wanted):
    return jax.vmap(lambda rows, chosen: rows[chosen])(table, wanted)


def pool_batch(requests, order, table):
    requests = requests[order]
    count = requests.shape[0]
    step = min(512, count)
    codes = jnp.arange(table.shape[1], dtype=jnp.int32)

    def one_block(lookup_block):
        counts = jnp.sum((lookup_block[..., None] == codes).astype(jnp.bfloat16), axis=2)
        return jnp.einsum("rfk,fke->rfe", counts, table, preferred_element_type=jnp.float32).astype(
            jnp.bfloat16
        )

    blocks = requests.reshape((count // step, step) + requests.shape[1:])
    pooled = lax.map(one_block, blocks)
    return pooled.reshape((count,) + pooled.shape[2:])


def on_device(
    cache,
    backing,
    resident,
    promote,
    victim,
    lookups,
    route,
    dcn_down,
    dcn_up,
    dcn_bias,
    mlp_in,
    mlp_bias,
    mlp_out,
    out_bias,
):
    held = cache.shape[0]
    slots = cache.shape[1]
    block = cache.shape[2]
    width = cache.shape[3]
    own_blocks = backing.shape[1]
    promoted_count = promote.shape[1]
    owner_here = lax.axis_index("owner")
    local_index = promote - owner_here * own_blocks
    owned_here = (local_index >= 0) & (local_index < own_blocks)
    clamped = jnp.clip(local_index, 0, own_blocks - 1)
    fetched = take_rows(backing, clamped)
    outgoing = jnp.where(owned_here[:, :, None, None], fetched, jnp.zeros_like(fetched))
    arrived = lax.all_gather(outgoing, "owner", axis=0, tiled=True)
    owners = arrived.shape[0] // held
    arrived = arrived.reshape(owners, held, promoted_count, block, width)
    source = promote // own_blocks
    picked = source[None] == jnp.arange(owners, dtype=jnp.int32)[:, None, None]
    promoted = jnp.sum(jnp.where(picked[..., None, None], arrived, jnp.zeros_like(arrived)), axis=0)
    evicted = take_rows(cache, victim)
    leaving = take_rows(resident, victim) - owner_here * own_blocks
    slot_numbers = jnp.arange(slots, dtype=jnp.int32)
    block_numbers = jnp.arange(own_blocks, dtype=jnp.int32)
    new_cache = cache
    new_backing = backing
    for column in range(promoted_count):
        slot_hit = victim[:, column][:, None] == slot_numbers[None, :]
        new_cache = jnp.where(slot_hit[:, :, None, None], promoted[:, column][:, None], new_cache)
        block_hit = leaving[:, column][:, None] == block_numbers[None, :]
        new_backing = jnp.where(
            block_hit[:, :, None, None], evicted[:, column][:, None], new_backing
        )
    table = new_cache.reshape(held, slots * block, width)
    batches = lookups.shape[0]
    received = []
    for batch_turn in range(batches):
        pooled = pool_batch(lookups[batch_turn], route[batch_turn, 0], table)
        received.append(lax.all_to_all(pooled, "cache", split_axis=0, concat_axis=1, tiled=True))
    arrived_rows = jnp.stack(received)
    per_batch = arrived_rows.shape[1]
    features = arrived_rows.reshape(batches * per_batch, -1)
    low = jnp.dot(
        features,
        lax.all_gather(dcn_down, "cache", axis=0, tiled=True),
        preferred_element_type=jnp.float32,
    ).astype(jnp.bfloat16)
    gate = (
        jnp.dot(
            low,
            lax.all_gather(dcn_up, "cache", axis=1, tiled=True),
            preferred_element_type=jnp.float32,
        )
        + dcn_bias
    )
    crossed = (features * gate + features).astype(jnp.bfloat16)
    portion = mlp_in.shape[1] // lax.axis_size("owner")
    own_columns = lax.dynamic_slice_in_dim(mlp_in, owner_here * portion, portion, 1)
    column_block = lax.all_gather(own_columns, "cache", axis=0, tiled=True)
    before = jnp.dot(
        crossed,
        lax.all_gather(column_block, "owner", axis=1, tiled=True),
        preferred_element_type=jnp.float32,
    )
    hidden = jnp.maximum(before + mlp_bias, 0.0)
    scores = jnp.sum(hidden * mlp_out, axis=-1) + out_bias[0]
    return (scores.reshape(batches, 1, per_batch), new_cache, new_backing)


def solution(mesh):
    in_specs = (
        P("cache", None, None, None),
        P("cache", "owner", None, None),
        P("cache", None),
        P("cache", None),
        P("cache", None),
        P(None, "owner", "cache", None),
        P(None, "owner", None),
        P("cache", None),
        P(None, "cache"),
        P(),
        P("cache", None),
        P(),
        P(),
        P(),
    )
    out_specs = (
        P(None, "owner", "cache"),
        P("cache", None, None, None),
        P("cache", "owner", None, None),
    )
    return jax.shard_map(
        on_device, mesh=mesh, in_specs=in_specs, out_specs=out_specs, check_vma=False
    )
```

profile of v0, /device:TPU:0, one launch (start us, length us, event | category | flops | bytes accessed | tf_op | source)
XLA Modules:
  0.0 392.6 jit_solution(9065323531690684591)
XLA Ops:
  11.4 2.2 gather_fusion.2
  15.8 70.4 %all-gather.12.cloned.1.call-done = bf16[8192,256]{1,0:T(8,128)(2,1)} async-done(((bf16[1024,256]{1,0:T(8,128)(2,1)}), bf16[8192,256]{1,0:T(8,128)(2,1)}) %all-gather.12.cloned.1.call-update) | async-done | bytes 4194320 | tf_op jit(solution)/shard_map/all_gather | solution.py:100
  88.1 7.9 %gather_fusion = s32[1024,4,8]{2,1,0:T(4,128)} fusion(s32[1024,4,8]{2,1,0:T(4,128)S(1)} %bitcast.100, s32[1024]{0:T(1024)S(1)} %broadcast_clamp_fusion.1), kind=kCustom, calls=%fused_computation | custom fusion | bytes 266240 | tf_op jit(solution)/shard_map/gather | solution.py:12
  96.0 1.8 copy.113
  98.0 10.9 %all-gather.6.cloned.1.call-done = bf16[16,2,128,256]{3,2,1,0:T(8,128)(2,1)} async-done(((bf16[4,2,128,256]{3,2,1,0:T(8,128)(2,1)}), bf16[16,2,128,256]{3,2,1,0:T(8,128)(2,1)}) %all-gather.6.cloned.1.call-update) | async-done | bytes 2097168 | tf_op jit(solution)/shard_map/all_gather | solution.py:56
  108.9 2.1 select_reduce_fusion
  113.7 27.7 %while.26 = (s32[]{:T(128)}, bf16[2,512,4,256]{3,1,0,2:T(8,128)(2,1)}, s32[2,512,4,8]{1,3,2,0:T(8,128)S(1)}, bf16[4,512,256]{2,1,0:T(8,128)(2,1)}, s32[]{:T(128)}) while((s32[]{:T(128)}, bf16[2,512,4,256]{3,1,0,2:T(8,128)(2,1)}, s32[2,512,4,8]{1,3,2,0:T(8,128)S(1)}, bf16[4,512,256]{2,1,0:T(8,128)(2,1)}, s32[]{:T(128)}) %tuple.91), condition=%wide.region_3.4_spmd.clone, body=%wide.region_1.3_spmd.clone.sunk | while | flops 561512448 | bytes 10814045 | solution.py:24
  114.2 11.7 %fusion.60 = bf16[512,4,512]{2,1,0:T(4,128)(2,1)S(1)} fusion(s32[512,4,8]{2,1,0:T(4,128)S(1)} %copy.164), kind=kLoop, calls=%fused_computation.9.clone.1 | loop fusion | flops 24117248 | bytes 2162688 | tf_op jit(solution)/shard_map/while/body/eval_jaxpr/reduce_sum | solution.py:18
  125.9 1.7 fusion.61
  128.0 11.7 %fusion.60 = bf16[512,4,512]{2,1,0:T(4,128)(2,1)S(1)} fusion(s32[512,4,8]{2,1,0:T(4,128)S(1)} %copy.164), kind=kLoop, calls=%fused_computation.9.clone.1 | loop fusion | flops 24117248 | bytes 2162688 | tf_op jit(solution)/shard_map/while/body/eval_jaxpr/reduce_sum | solution.py:18
  139.8 1.7 fusion.61
  141.5 4.5 %copy.115 = bf16[1024,4,256]{2,1,0:T(4,128)(2,1)} copy(bf16[1024,4,256]{2,0,1:T(8,128)(2,1)} %bitcast.12) | data formatting | bytes 4194304 | tf_op jit(solution)/shard_map/reshape | solution.py:25
  146.0 5.5 %all-to-all-start = ((bf16[1024,4,256]{2,1,0:T(4,128)(2,1)}), bf16[1024,4,256]{2,1,0:T(4,128)(2,1)}, u32[]{:S(2)}, u32[]{:S(2)}) async-start(bf16[1024,4,256]{2,1,0:T(4,128)(2,1)} %copy.115), calls=%async_computation | async-start | bytes 4194304 | tf_op jit(solution)/shard_map/all_to_all | solution.py:80
  152.3 7.9 %gather_fusion.1 = s32[1024,4,8]{2,1,0:T(4,128)} fusion(s32[1024,4,8]{2,1,0:T(4,128)S(1)} %bitcast.101, s32[1024]{0:T(1024)S(1)} %broadcast_clamp_fusion), kind=kCustom, calls=%fused_computation.1 | custom fusion | bytes 266240 | tf_op jit(solution)/shard_map/gather | solution.py:12
  160.3 1.8 copy.120
  163.6 27.7 %while.27 = (s32[]{:T(128)}, bf16[2,512,4,256]{3,1,0,2:T(8,128)(2,1)}, s32[2,512,4,8]{1,3,2,0:T(8,128)S(1)}, bf16[4,512,256]{2,1,0:T(8,128)(2,1)}, s32[]{:T(128)}) while((s32[]{:T(128)}, bf16[2,512,4,256]{3,1,0,2:T(8,128)(2,1)}, s32[2,512,4,8]{1,3,2,0:T(8,128)S(1)}, bf16[4,512,256]{2,1,0:T(8,128)(2,1)}, s32[]{:T(128)}) %tuple.92), condition=%wide.region_6.7_spmd.clone, body=%wide.region_4.6_spmd.clone.sunk | while | flops 561512448 | bytes 10814045 | solution.py:24
  164.0 11.7 %fusion.64 = bf16[512,4,512]{2,1,0:T(4,128)(2,1)S(1)} fusion(s32[512,4,8]{2,1,0:T(4,128)S(1)} %copy.166), kind=kLoop, calls=%fused_computation.18.clone.1 | loop fusion | flops 24117248 | bytes 2162688 | tf_op jit(solution)/shard_map/while/body/eval_jaxpr/reduce_sum | solution.py:18
  175.7 1.7 fusion.65
  177.9 11.7 %fusion.64 = bf16[512,4,512]{2,1,0:T(4,128)(2,1)S(1)} fusion(s32[512,4,8]{2,1,0:T(4,128)S(1)} %copy.166), kind=kLoop, calls=%fused_computation.18.clone.1 | loop fusion | flops 24117248 | bytes 2162688 | tf_op jit(solution)/shard_map/while/body/eval_jaxpr/reduce_sum | solution.py:18
  189.6 1.7 fusion.65
  191.3 4.6 %copy.122 = bf16[1024,4,256]{2,1,0:T(4,128)(2,1)} copy(bf16[1024,4,256]{2,0,1:T(8,128)(2,1)} %bitcast.20) | data formatting | bytes 4194304 | tf_op jit(solution)/shard_map/reshape | solution.py:25
  195.9 17.7 %all-to-all-done = bf16[1024,4,256]{2,1,0:T(4,128)(2,1)} async-done(((bf16[1024,4,256]{2,1,0:T(4,128)(2,1)}), bf16[1024,4,256]{2,1,0:T(4,128)(2,1)}, u32[]{:S(2)}, u32[]{:S(2)}) %all-to-all-start) | async-done | bytes 2097184 | tf_op jit(solution)/shard_map/all_to_all | solution.py:80
  213.6 4.6 %all-to-all-start.1 = ((bf16[1024,4,256]{2,1,0:T(4,128)(2,1)}), bf16[1024,4,256]{2,1,0:T(4,128)(2,1)}, u32[]{:S(2)}, u32[]{:S(2)}) async-start(bf16[1024,4,256]{2,1,0:T(4,128)(2,1)} %copy.122), calls=%async_computation.1 | async-start | bytes 4194304 | tf_op jit(solution)/shard_map/all_to_all | solution.py:80
  220.7 3.3 select_select_fusion
  224.0 1.9 copy.116
  227.4 53.9 %all-to-all-done.1 = bf16[1024,4,256]{2,1,0:T(4,128)(2,1)} async-done(((bf16[1024,4,256]{2,1,0:T(4,128)(2,1)}), bf16[1024,4,256]{2,1,0:T(4,128)(2,1)}, u32[]{:S(2)}, u32[]{:S(2)}) %all-to-all-start.1) | async-done | bytes 2097184 | tf_op jit(solution)/shard_map/all_to_all | solution.py:80
  281.3 1.9 copy.123
  285.3 2.4 copy.125
  287.7 6.3 %copy.142 = bf16[32,8,32,256]{3,1,2,0:T(8,128)(2,1)} copy(bf16[32,8,32,256]{3,2,1,0:T(8,128)(2,1)S(1)} %bitcast.99) | data formatting | bytes 8388608
  294.0 4.3 %convolution_convert_fusion = bf16[256,128]{1,0:T(8,128)(2,1)S(1)} fusion(bf16[256,8192]{1,0:T(8,128)(2,1)} %bitcast.97, bf16[8192,128]{1,0:T(8,128)(2,1)} %all-gather.8.cloned.1.call-done), kind=kOutput, calls=%fused_computation.35 | convolution fusion | flops 536903680 | bytes 6356992 | tf_op jit(solution)/shard_map/dot_general | solution.py:84
  298.3 74.4 %all-gather.14.cloned.1.call-done = bf16[8192,1024]{1,0:T(8,128)(2,1)} async-done(((bf16[8192,256]{1,0:T(8,128)(2,1)}), bf16[8192,1024]{1,0:T(8,128)(2,1)}) %all-gather.14.cloned.1.call-update) | async-done | bytes 16777232 | tf_op jit(solution)/shard_map/all_gather | solution.py:103
  372.7 12.8 %fusion.33 = f32[256]{0:T(256)S(1)} fusion(bf16[8192,1024]{1,0:T(8,128)(2,1)} %all-gather.14.cloned.1.call-done, bf16[256,128]{1,0:T(8,128)(2,1)S(1)} %convolution_convert_fusion, bf16[128,8192]{1,0:T(8,128)(2,1)} %all-gather.10.cloned.1.call-done, bf16[256,8192]{1,0:T(8,128)(2,1)} %bitcast.98, f32[8192]{0:T(1024)S(1)} %copy-done.12, ...), kind=kOutput, calls=%fused_computation.34 | convolution fusion | flops 4843372544 | bytes 23176192 | tf_op jit(solution)/shard_map/dot_general | solution.py:101
  (90 shorter events, 20.9 us)
Async XLA Ops:
  7.2 1.6 copy-start
  7.2 79.0 %all-gather.12.cloned.1.call-start = ((), (), s32[]{:S(2)}) async-start(), calls=%async_computation.5 | async-start | bytes 4718592 | tf_op jit(solution)/shard_map/all_gather | solution.py:100
  9.6 99.3 %all-gather.6.cloned.1.call-start = ((), (), s32[]{:S(2)}) async-start(), calls=%async_computation.2 | async-start | bytes 2621440 | tf_op jit(solution)/shard_map/all_gather | solution.py:56
  14.5 279.5 %all-gather.8.cloned.1.call-start = ((), (), s32[]{:S(2)}) async-start(), calls=%async_computation.3 | async-start | bytes 2359296 | tf_op jit(solution)/shard_map/all_gather | solution.py:86
  15.2 283.1 %all-gather.10.cloned.1.call-start = ((), (), s32[]{:S(2)}) async-start(), calls=%async_computation.4 | async-start | bytes 2359296 | tf_op jit(solution)/shard_map/all_gather | solution.py:92
  15.8 356.9 %all-gather.14.cloned.1.call-start = ((), (), s32[]{:S(2)}) async-start(), calls=%async_computation.6 | async-start | bytes 20971520 | tf_op jit(solution)/shard_map/all_gather | solution.py:103
  86.2 0.7 copy-start.9
  86.2 1.0 copy-start.8
  86.3 1.8 copy-start.10
  96.0 1.9 copy-start.11
  97.9 13.2 %copy-start.4 = (bf16[4,4,128,256]{3,2,1,0:T(8,128)(2,1)S(1)}, bf16[4,4,128,256]{3,2,1,0:T(8,128)(2,1)}, u32[]{:S(2)}) copy-start(bf16[4,4,128,256]{3,2,1,0:T(8,128)(2,1)} %param.18) | copy-start | bytes 3145732
  114.2 11.7 %copy-start.6 = (bf16[4,512,256]{2,1,0:T(8,128)(2,1)S(1)}, bf16[4,512,256]{2,1,0:T(8,128)(2,1)}, u32[]{:S(2)}) copy-start(bf16[4,512,256]{2,1,0:T(8,128)(2,1)} %get-tuple-element.305) | copy-start | bytes 3145732 | tf_op jit(solution)/shard_map/while
  128.0 11.7 %copy-start.6 = (bf16[4,512,256]{2,1,0:T(8,128)(2,1)S(1)}, bf16[4,512,256]{2,1,0:T(8,128)(2,1)}, u32[]{:S(2)}) copy-start(bf16[4,512,256]{2,1,0:T(8,128)(2,1)} %get-tuple-element.305) | copy-start | bytes 3145732 | tf_op jit(solution)/shard_map/while
  146.0 67.6 %all-to-all-start = ((bf16[1024,4,256]{2,1,0:T(4,128)(2,1)}), bf16[1024,4,256]{2,1,0:T(4,128)(2,1)}, u32[]{:S(2)}, u32[]{:S(2)}) async-start(bf16[1024,4,256]{2,1,0:T(4,128)(2,1)} %copy.115), calls=%async_computation | async-start | bytes 4194304 | tf_op jit(solution)/shard_map/all_to_all | solution.py:80
  164.0 11.7 %copy-start.7 = (bf16[4,512,256]{2,1,0:T(8,128)(2,1)S(1)}, bf16[4,512,256]{2,1,0:T(8,128)(2,1)}, u32[]{:S(2)}) copy-start(bf16[4,512,256]{2,1,0:T(8,128)(2,1)} %get-tuple-element.290) | copy-start | bytes 3145732 | tf_op jit(solution)/shard_map/while
  177.8 11.7 %copy-start.7 = (bf16[4,512,256]{2,1,0:T(8,128)(2,1)S(1)}, bf16[4,512,256]{2,1,0:T(8,128)(2,1)}, u32[]{:S(2)}) copy-start(bf16[4,512,256]{2,1,0:T(8,128)(2,1)} %get-tuple-element.290) | copy-start | bytes 3145732 | tf_op jit(solution)/shard_map/while
  195.9 23.1 %copy-start.5 = (bf16[4,4,128,256]{3,2,1,0:T(8,128)(2,1)S(1)}, bf16[4,4,128,256]{3,2,1,0:T(8,128)(2,1)}, u32[]{:S(2)}) copy-start(bf16[4,4,128,256]{3,2,1,0:T(8,128)(2,1)} %param.18) | copy-start | bytes 3145732
  195.9 23.7 %copy-start.2 = (s32[4,4]{1,0:T(4,128)S(1)}, s32[4,4]{1,0:T(4,128)}, u32[]{:S(2)}) copy-start(s32[4,4]{1,0:T(4,128)} %param.20) | copy-start | bytes 196
  213.6 67.7 %all-to-all-start.1 = ((bf16[1024,4,256]{2,1,0:T(4,128)(2,1)}), bf16[1024,4,256]{2,1,0:T(4,128)(2,1)}, u32[]{:S(2)}, u32[]{:S(2)}) async-start(bf16[1024,4,256]{2,1,0:T(4,128)(2,1)} %copy.122), calls=%async_computation.1 | async-start | bytes 4194304 | tf_op jit(solution)/shard_map/all_to_all | solution.py:80
  283.2 1.6 copy-start.3
  294.0 78.7 %copy-start.12 = (f32[8192]{0:T(1024)S(1)}, f32[8192]{0:T(1024)}, u32[]{:S(2)}) copy-start(f32[8192]{0:T(1024)} %param.27) | copy-start | bytes 98308
  294.0 78.7 %copy-start.13 = (f32[1024]{0:T(1024)S(1)}, f32[1024]{0:T(1024)}, u32[]{:S(2)}) copy-start(f32[1024]{0:T(1024)} %param.30) | copy-start | bytes 12292
  294.0 78.7 %copy-start.14 = (f32[1024]{0:T(1024)S(1)}, f32[1024]{0:T(1024)}, u32[]{:S(2)}) copy-start(f32[1024]{0:T(1024)} %param.29) | copy-start | bytes 12292
  372.7 13.3 %copy-start.1 = (bf16[1024,1024]{1,0:T(8,128)(2,1)S(1)}, bf16[1024,1024]{1,0:T(8,128)(2,1)}, u32[]{:S(2)}) copy-start(bf16[1024,1024]{1,0:T(8,128)(2,1)} %param.28) | copy-start | bytes 6291460
Sparse Core Ops, SparseCore 0:
  10.7 75.4 all-gather.11
  87.8 21.0 all-gather.5
  111.1 52.2 all-gather.7
  165.3 89.3 all-gather.9
  256.1 116.5 all-gather.13
where the time goes:
time: 393 us
  waiting for transfers between devices  229 us (58%)
  local copies, waits for them, and re-layouts  58.2 us (15%)
  other arithmetic  56.9 us (14%)
  matrix products  23.8 us (6%)
  between operations  14.7 us (4%)
  starting transfers between devices  10.3 us (3%)
    all_gather x1, waiting for transfers between devices, on_device(): lax.all_gather(column_block, 'owner', axis=1, tiled=True)  74.4 us
    all_to_all x2, waiting for transfers between devices, on_device(): lax.all_to_all(pooled, 'cache', split_axis=0, concat_axis=1, tiled=True)  71.6 us
    all_gather x1, waiting for transfers between devices, on_device(): column_block = lax.all_gather(own_columns, 'cache', axis=0, tiled=True)  70.4 us
    reduce_sum x4, other arithmetic, one_block(): jnp.sum((lookup_block[..., None] == codes).astype(jnp.bfloat16), axis=2)  46.9 us
    gather x2, local copies, waits for them, and re-layouts, pool_batch(): requests = requests[order]  15.9 us
    unnamed x31, local copies, waits for them, and re-layouts  15.5 us
    dot_general x1, matrix products, on_device(): jnp.dot(crossed, lax.all_gather(column_block, 'owner', axis=1, tiled=True...  12.8 us
    all_gather x1, waiting for transfers between devices, on_device(): arrived = lax.all_gather(outgoing, 'owner', axis=0, tiled=True)  10.9 us
  transfers between devices with their start and end apart: 7, of which 5 were waited for; matrix products, arithmetic and copies ran while one was open for 31% of the time, Pallas kernels for 0%

commit v1 on v0

--- a/solution.py
+++ b/solution.py
@@ -100,7 +100,7 @@
     column_block = lax.all_gather(own_columns, "cache", axis=0, tiled=True)
     before = jnp.dot(
         crossed,
-        lax.all_gather(column_block, "owner", axis=1, tiled=True),
+        jnp.concatenate(lax.all_gather(column_block, "owner"), axis=1),
         preferred_element_type=jnp.float32,
     )
     hidden = jnp.maximum(before + mlp_bias, 0.0)

time: 393 us -> 352 us (0.90)
  waiting for transfers between devices: 229 us -> 164 us
  local copies, waits for them, and re-layouts: 58.2 us -> 85.4 us
  matrix products: 23.8 us -> 19.7 us
    all_gather x1, waiting for transfers between devices: 74.4 us -> 5 us  [on_device(): lax.all_gather(column_block, 'owner')]
    all_gather x1, waiting for transfers between devices: 0.02 us -> 29.4 us  [on_device(): lax.all_gather(dcn_up, 'cache', axis=1, tiled=True)]
    all_to_all x2, waiting for transfers between devices: 71.6 us -> 46.4 us  [on_device(): lax.all_to_all(pooled, 'cache', split_axis=0, concat_axis=1, tiled=True)]
    reshape x0 -> x1, local copies, waits for them, and re-layouts: none -> 21.7 us  [on_device(): jnp.concatenate(lax.all_gather(column_block, 'owner'), axis=1)]
    while x8 -> x24, local copies, waits for them, and re-layouts: 0.03 us -> 5.31 us
  transfers between devices with their start and end apart: 7 -> 7, of which waited for: 5 -> 6; matrix products, arithmetic and copies ran while one was open for 31% -> 40% of each run, Pallas kernels for 0% -> 0%
where the time goes in v1:
time: 352 us; the launch traced here: 351 us
  waiting for transfers between devices  164 us (47%)
  local copies, waits for them, and re-layouts  85.4 us (24%)
  other arithmetic  57 us (16%)
  matrix products  19.7 us (6%)
  between operations  14.7 us (4%)
  starting transfers between devices  10.3 us (3%)
    all_gather x1, waiting for transfers between devices, on_device(): column_block = lax.all_gather(own_columns, 'cache', axis=0, tiled=True)  70.9 us
    reduce_sum x4, other arithmetic, one_block(): jnp.sum((lookup_block[..., None] == codes).astype(jnp.bfloat16), axis=2)  46.9 us
    all_to_all x2, waiting for transfers between devices, on_device(): lax.all_to_all(pooled, 'cache', split_axis=0, concat_axis=1, tiled=True)  46.4 us
    all_gather x1, waiting for transfers between devices, on_device(): lax.all_gather(dcn_up, 'cache', axis=1, tiled=True)  29.4 us
    reshape x1, local copies, waits for them, and re-layouts, on_device(): jnp.concatenate(lax.all_gather(column_block, 'owner'), axis=1)  21.7 us
    gather x2, local copies, waits for them, and re-layouts, pool_batch(): requests = requests[order]  15.9 us
    unnamed x31, local copies, waits for them, and re-layouts  15.6 us
    dot_general x1, matrix products, on_device(): jnp.dot(crossed, jnp.concatenate(lax.all_gather(column_block, 'owner'), a...  12.7 us
  transfers between devices with their start and end apart: 7, of which 6 were waited for; matrix products, arithmetic and copies ran while one was open for 40% of the time, Pallas kernels for 0%

profile of v1, /device:TPU:0, one launch (start us, length us, event | category | flops | bytes accessed | tf_op | source)
XLA Modules:
  0.0 350.8 jit_solution(13821655663095036658)
XLA Ops:
  7.2 1.5 copy-done
  11.4 2.2 gather_fusion.2
  15.4 70.9 %all-gather.13.cloned.1.call-done = bf16[8192,256]{1,0:T(8,128)(2,1)} async-done(((bf16[1024,256]{1,0:T(8,128)(2,1)}), bf16[8192,256]{1,0:T(8,128)(2,1)}) %all-gather.13.cloned.1.call-update) | async-done | bytes 4194320 | tf_op jit(solution)/shard_map/all_gather | solution.py:100
  88.1 7.9 %gather_fusion.1 = s32[1024,4,8]{2,1,0:T(4,128)} fusion(s32[1024,4,8]{2,1,0:T(4,128)S(1)} %bitcast.106, s32[1024]{0:T(1024)S(1)} %broadcast_clamp_fusion), kind=kCustom, calls=%fused_computation.1 | custom fusion | bytes 266240 | tf_op jit(solution)/shard_map/gather | solution.py:12
  96.0 1.9 copy.123
  98.1 10.8 %all-gather.7.cloned.1.call-done = bf16[16,2,128,256]{3,2,1,0:T(8,128)(2,1)} async-done(((bf16[4,2,128,256]{3,2,1,0:T(8,128)(2,1)}), bf16[16,2,128,256]{3,2,1,0:T(8,128)(2,1)}) %all-gather.7.cloned.1.call-update) | async-done | bytes 2097168 | tf_op jit(solution)/shard_map/all_gather | solution.py:56
  108.9 2.1 select_reduce_fusion
  113.7 28.5 %while.27 = (s32[]{:T(128)}, bf16[2,512,4,256]{3,1,0,2:T(8,128)(2,1)}, s32[2,512,4,8]{1,3,2,0:T(8,128)S(1)}, bf16[4,512,256]{2,1,0:T(8,128)(2,1)}, s32[]{:T(128)}) while((s32[]{:T(128)}, bf16[2,512,4,256]{3,1,0,2:T(8,128)(2,1)}, s32[2,512,4,8]{1,3,2,0:T(8,128)S(1)}, bf16[4,512,256]{2,1,0:T(8,128)(2,1)}, s32[]{:T(128)}) %tuple.91), condition=%wide.region_6.7_spmd.clone, body=%wide.region_4.6_spmd.clone.sunk | while | flops 561512448 | bytes 27590816 | solution.py:24
  114.2 11.7 %fusion.64 = bf16[512,4,512]{2,1,0:T(4,128)(2,1)S(1)} fusion(s32[512,4,8]{2,1,0:T(4,128)S(1)} %copy.170), kind=kLoop, calls=%fused_computation.18.clone.1 | loop fusion | flops 24117248 | bytes 2162688 | tf_op jit(solution)/shard_map/while/body/eval_jaxpr/reduce_sum | solution.py:18
  128.4 11.7 %fusion.64 = bf16[512,4,512]{2,1,0:T(4,128)(2,1)S(1)} fusion(s32[512,4,8]{2,1,0:T(4,128)S(1)} %copy.170), kind=kLoop, calls=%fused_computation.18.clone.1 | loop fusion | flops 24117248 | bytes 2162688 | tf_op jit(solution)/shard_map/while/body/eval_jaxpr/reduce_sum | solution.py:18
  142.2 4.6 %copy.125 = bf16[1024,4,256]{2,1,0:T(4,128)(2,1)} copy(bf16[1024,4,256]{2,0,1:T(8,128)(2,1)} %bitcast.111) | data formatting | bytes 4194304 | tf_op jit(solution)/shard_map/reshape | solution.py:25
  146.8 5.5 %all-to-all-start.1 = ((bf16[1024,4,256]{2,1,0:T(4,128)(2,1)}), bf16[1024,4,256]{2,1,0:T(4,128)(2,1)}, u32[]{:S(2)}, u32[]{:S(2)}) async-start(bf16[1024,4,256]{2,1,0:T(4,128)(2,1)} %copy.125), calls=%async_computation.1 | async-start | bytes 4194304 | tf_op jit(solution)/shard_map/all_to_all | solution.py:80
  153.2 7.9 %gather_fusion = s32[1024,4,8]{2,1,0:T(4,128)} fusion(s32[1024,4,8]{2,1,0:T(4,128)S(1)} %bitcast.107, s32[1024]{0:T(1024)S(1)} %broadcast_clamp_fusion.1), kind=kCustom, calls=%fused_computation | custom fusion | bytes 266240 | tf_op jit(solution)/shard_map/gather | solution.py:12
  161.1 1.8 copy.116
  164.4 28.5 %while.26 = (s32[]{:T(128)}, bf16[2,512,4,256]{3,1,0,2:T(8,128)(2,1)}, s32[2,512,4,8]{1,3,2,0:T(8,128)S(1)}, bf16[4,512,256]{2,1,0:T(8,128)(2,1)}, s32[]{:T(128)}) while((s32[]{:T(128)}, bf16[2,512,4,256]{3,1,0,2:T(8,128)(2,1)}, s32[2,512,4,8]{1,3,2,0:T(8,128)S(1)}, bf16[4,512,256]{2,1,0:T(8,128)(2,1)}, s32[]{:T(128)}) %tuple.92), condition=%wide.region_3.4_spmd.clone, body=%wide.region_1.3_spmd.clone.sunk | while | flops 561512448 | bytes 27590816 | solution.py:24
  164.8 11.7 %fusion.60 = bf16[512,4,512]{2,1,0:T(4,128)(2,1)S(1)} fusion(s32[512,4,8]{2,1,0:T(4,128)S(1)} %copy.168), kind=kLoop, calls=%fused_computation.9.clone.1 | loop fusion | flops 24117248 | bytes 2162688 | tf_op jit(solution)/shard_map/while/body/eval_jaxpr/reduce_sum | solution.py:18
  179.1 11.7 %fusion.60 = bf16[512,4,512]{2,1,0:T(4,128)(2,1)S(1)} fusion(s32[512,4,8]{2,1,0:T(4,128)S(1)} %copy.168), kind=kLoop, calls=%fused_computation.9.clone.1 | loop fusion | flops 24117248 | bytes 2162688 | tf_op jit(solution)/shard_map/while/body/eval_jaxpr/reduce_sum | solution.py:18
  192.9 4.6 %copy.118 = bf16[1024,4,256]{2,1,0:T(4,128)(2,1)} copy(bf16[1024,4,256]{2,0,1:T(8,128)(2,1)} %bitcast.110) | data formatting | bytes 4194304 | tf_op jit(solution)/shard_map/reshape | solution.py:25
  197.5 7.6 %all-to-all-done.1 = bf16[1024,4,256]{2,1,0:T(4,128)(2,1)} async-done(((bf16[1024,4,256]{2,1,0:T(4,128)(2,1)}), bf16[1024,4,256]{2,1,0:T(4,128)(2,1)}, u32[]{:S(2)}, u32[]{:S(2)}) %all-to-all-start.1) | async-done | bytes 2097184 | tf_op jit(solution)/shard_map/all_to_all | solution.py:80
  205.1 4.4 %all-to-all-start = ((bf16[1024,4,256]{2,1,0:T(4,128)(2,1)}), bf16[1024,4,256]{2,1,0:T(4,128)(2,1)}, u32[]{:S(2)}, u32[]{:S(2)}) async-start(bf16[1024,4,256]{2,1,0:T(4,128)(2,1)} %copy.118), calls=%async_computation | async-start | bytes 4194304 | tf_op jit(solution)/shard_map/all_to_all | solution.py:80
  212.6 3.2 select_select_fusion
  215.9 1.9 copy.126
  217.7 1.6 copy.127
  219.3 38.8 %all-to-all-done = bf16[1024,4,256]{2,1,0:T(4,128)(2,1)} async-done(((bf16[1024,4,256]{2,1,0:T(4,128)(2,1)}), bf16[1024,4,256]{2,1,0:T(4,128)(2,1)}, u32[]{:S(2)}, u32[]{:S(2)}) %all-to-all-start) | async-done | bytes 2097184 | tf_op jit(solution)/shard_map/all_to_all | solution.py:80
  258.1 1.9 copy.119
  262.0 2.4 copy.128
  264.4 6.3 %copy.146 = bf16[32,8,32,256]{3,1,2,0:T(8,128)(2,1)} copy(bf16[32,8,32,256]{3,2,1,0:T(8,128)(2,1)S(1)} %bitcast.105) | data formatting | bytes 8388608
  270.8 4.1 %convolution_convert_fusion = bf16[256,128]{1,0:T(8,128)(2,1)S(1)} fusion(bf16[256,8192]{1,0:T(8,128)(2,1)} %bitcast.103, bf16[8192,128]{1,0:T(8,128)(2,1)} %all-gather.9.cloned.1.call-done), kind=kOutput, calls=%fused_computation.35 | convolution fusion | flops 536903680 | bytes 6356992 | tf_op jit(solution)/shard_map/dot_general | solution.py:84
  274.9 5.0 %all-gather.15.cloned.1.call-done = bf16[32768,256]{1,0:T(8,128)(2,1)} async-done(((bf16[8192,256]{1,0:T(8,128)(2,1)}), bf16[32768,256]{1,0:T(8,128)(2,1)}) %all-gather.15.cloned.1.call-update) | async-done | bytes 16777232 | tf_op jit(solution)/shard_map/all_gather | solution.py:103
  279.9 21.7 %copy.129 = bf16[8192,4,256]{0,2,1:T(8,128)(2,1)} copy(bf16[8192,4,256]{2,0,1:T(8,128)(2,1)} %bitcast.101) | data formatting | bytes 33554432 | tf_op jit(solution)/shard_map/reshape | solution.py:103
  301.6 29.4 %all-gather.11.cloned.1.call-done = bf16[128,8192]{1,0:T(8,128)(2,1)} async-done(((bf16[128,1024]{1,0:T(8,128)(2,1)}), bf16[128,8192]{1,0:T(8,128)(2,1)}) %all-gather.11.cloned.1.call-update) | async-done | bytes 2097168 | tf_op jit(solution)/shard_map/all_gather | solution.py:92
  331.0 12.7 %fusion.33 = f32[256]{0:T(256)S(1)} fusion(bf16[8192,1024]{0,1:T(8,128)(2,1)} %bitcast.102, bf16[256,128]{1,0:T(8,128)(2,1)S(1)} %convolution_convert_fusion, bf16[128,8192]{1,0:T(8,128)(2,1)} %all-gather.11.cloned.1.call-done, bf16[256,8192]{1,0:T(8,128)(2,1)} %bitcast.104, f32[8192]{0:T(1024)S(1)} %copy-done.16, f32[1024]{0:T(1024)S(1)} %copy-done.17, ...), kind=kOutput, calls=%fused_computation.34 | convolution fusion | flops 4843372544 | bytes 23176192 | tf_op jit(solution)/shard_map/dot_general | solution.py:101
  (107 shorter events, 26.1 us)
Async XLA Ops:
  7.2 1.6 copy-start
  7.2 79.0 %all-gather.13.cloned.1.call-start = ((), (), s32[]{:S(2)}) async-start(), calls=%async_computation.5 | async-start | bytes 4718592 | tf_op jit(solution)/shard_map/all_gather | solution.py:100
  9.6 99.3 %all-gather.7.cloned.1.call-start = ((), (), s32[]{:S(2)}) async-start(), calls=%async_computation.2 | async-start | bytes 2621440 | tf_op jit(solution)/shard_map/all_gather | solution.py:56
  14.6 256.2 %all-gather.9.cloned.1.call-start = ((), (), s32[]{:S(2)}) async-start(), calls=%async_computation.3 | async-start | bytes 2359296 | tf_op jit(solution)/shard_map/all_gather | solution.py:86
  15.3 264.6 %all-gather.15.cloned.1.call-start = ((), (), s32[]{:S(2)}) async-start(), calls=%async_computation.6 | async-start | bytes 20971520 | tf_op jit(solution)/shard_map/all_gather | solution.py:103
  86.2 0.9 copy-start.12
  86.3 1.8 copy-start.14
  96.0 1.9 copy-start.13
  96.0 2.0 copy-start.15
  97.9 13.2 %copy-start.8 = (bf16[4,4,128,256]{3,2,1,0:T(8,128)(2,1)S(1)}, bf16[4,4,128,256]{3,2,1,0:T(8,128)(2,1)}, u32[]{:S(2)}) copy-start(bf16[4,4,128,256]{3,2,1,0:T(8,128)(2,1)} %param.18) | copy-start | bytes 3145732
  114.2 11.8 %copy-start.5 = (bf16[2,512,4,256]{3,1,0,2:T(8,128)(2,1)S(1)}, bf16[2,512,4,256]{3,1,0,2:T(8,128)(2,1)}, u32[]{:S(2)}) copy-start(bf16[2,512,4,256]{3,1,0,2:T(8,128)(2,1)} %get-tuple-element.283) | copy-start | bytes 6291460 | tf_op jit(solution)/shard_map/while
  114.2 11.8 %copy-start.10 = (bf16[4,512,256]{2,1,0:T(8,128)(2,1)S(1)}, bf16[4,512,256]{2,1,0:T(8,128)(2,1)}, u32[]{:S(2)}) copy-start(bf16[4,512,256]{2,1,0:T(8,128)(2,1)} %get-tuple-element.290) | copy-start | bytes 3145732 | tf_op jit(solution)/shard_map/while
  126.7 1.3 copy-start.6
  128.4 11.8 %copy-start.5 = (bf16[2,512,4,256]{3,1,0,2:T(8,128)(2,1)S(1)}, bf16[2,512,4,256]{3,1,0,2:T(8,128)(2,1)}, u32[]{:S(2)}) copy-start(bf16[2,512,4,256]{3,1,0,2:T(8,128)(2,1)} %get-tuple-element.283) | copy-start | bytes 6291460 | tf_op jit(solution)/shard_map/while
  128.4 11.8 %copy-start.10 = (bf16[4,512,256]{2,1,0:T(8,128)(2,1)S(1)}, bf16[4,512,256]{2,1,0:T(8,128)(2,1)}, u32[]{:S(2)}) copy-start(bf16[4,512,256]{2,1,0:T(8,128)(2,1)} %get-tuple-element.290) | copy-start | bytes 3145732 | tf_op jit(solution)/shard_map/while
  140.9 1.3 copy-start.6
  146.8 58.3 %all-to-all-start.1 = ((bf16[1024,4,256]{2,1,0:T(4,128)(2,1)}), bf16[1024,4,256]{2,1,0:T(4,128)(2,1)}, u32[]{:S(2)}, u32[]{:S(2)}) async-start(bf16[1024,4,256]{2,1,0:T(4,128)(2,1)} %copy.125), calls=%async_computation.1 | async-start | bytes 4194304 | tf_op jit(solution)/shard_map/all_to_all | solution.py:80
  164.8 11.8 %copy-start.3 = (bf16[2,512,4,256]{3,1,0,2:T(8,128)(2,1)S(1)}, bf16[2,512,4,256]{3,1,0,2:T(8,128)(2,1)}, u32[]{:S(2)}) copy-start(bf16[2,512,4,256]{3,1,0,2:T(8,128)(2,1)} %get-tuple-element.298) | copy-start | bytes 6291460 | tf_op jit(solution)/shard_map/while
  164.8 11.8 %copy-start.11 = (bf16[4,512,256]{2,1,0:T(8,128)(2,1)S(1)}, bf16[4,512,256]{2,1,0:T(8,128)(2,1)}, u32[]{:S(2)}) copy-start(bf16[4,512,256]{2,1,0:T(8,128)(2,1)} %get-tuple-element.305) | copy-start | bytes 3145732 | tf_op jit(solution)/shard_map/while
  177.3 1.3 copy-start.4
  179.0 11.8 %copy-start.3 = (bf16[2,512,4,256]{3,1,0,2:T(8,128)(2,1)S(1)}, bf16[2,512,4,256]{3,1,0,2:T(8,128)(2,1)}, u32[]{:S(2)}) copy-start(bf16[2,512,4,256]{3,1,0,2:T(8,128)(2,1)} %get-tuple-element.298) | copy-start | bytes 6291460 | tf_op jit(solution)/shard_map/while
  179.0 11.8 %copy-start.11 = (bf16[4,512,256]{2,1,0:T(8,128)(2,1)S(1)}, bf16[4,512,256]{2,1,0:T(8,128)(2,1)}, u32[]{:S(2)}) copy-start(bf16[4,512,256]{2,1,0:T(8,128)(2,1)} %get-tuple-element.305) | copy-start | bytes 3145732 | tf_op jit(solution)/shard_map/while
  191.5 1.3 copy-start.4
  197.5 13.4 %copy-start.9 = (bf16[4,4,128,256]{3,2,1,0:T(8,128)(2,1)S(1)}, bf16[4,4,128,256]{3,2,1,0:T(8,128)(2,1)}, u32[]{:S(2)}) copy-start(bf16[4,4,128,256]{3,2,1,0:T(8,128)(2,1)} %param.18) | copy-start | bytes 3145732
  197.5 14.0 %copy-start.2 = (s32[4,4]{1,0:T(4,128)S(1)}, s32[4,4]{1,0:T(4,128)}, u32[]{:S(2)}) copy-start(s32[4,4]{1,0:T(4,128)} %param.20) | copy-start | bytes 196
  205.1 53.0 %all-to-all-start = ((bf16[1024,4,256]{2,1,0:T(4,128)(2,1)}), bf16[1024,4,256]{2,1,0:T(4,128)(2,1)}, u32[]{:S(2)}, u32[]{:S(2)}) async-start(bf16[1024,4,256]{2,1,0:T(4,128)(2,1)} %copy.118), calls=%async_computation | async-start | bytes 4194304 | tf_op jit(solution)/shard_map/all_to_all | solution.py:80
  209.5 121.5 %all-gather.11.cloned.1.call-start = ((), (), s32[]{:S(2)}) async-start(), calls=%async_computation.4 | async-start | bytes 2359296 | tf_op jit(solution)/shard_map/all_gather | solution.py:92
  260.0 1.6 copy-start.7
  279.9 51.1 %copy-start.16 = (f32[8192]{0:T(1024)S(1)}, f32[8192]{0:T(1024)}, u32[]{:S(2)}) copy-start(f32[8192]{0:T(1024)} %param.27) | copy-start | bytes 98308
  279.9 51.1 %copy-start.17 = (f32[1024]{0:T(1024)S(1)}, f32[1024]{0:T(1024)}, u32[]{:S(2)}) copy-start(f32[1024]{0:T(1024)} %param.30) | copy-start | bytes 12292
  279.9 51.1 %copy-start.18 = (f32[1024]{0:T(1024)S(1)}, f32[1024]{0:T(1024)}, u32[]{:S(2)}) copy-start(f32[1024]{0:T(1024)} %param.29) | copy-start | bytes 12292
  331.0 13.3 %copy-start.1 = (bf16[1024,1024]{1,0:T(8,128)(2,1)S(1)}, bf16[1024,1024]{1,0:T(8,128)(2,1)}, u32[]{:S(2)}) copy-start(bf16[1024,1024]{1,0:T(8,128)(2,1)} %param.28) | copy-start | bytes 6291460
Sparse Core Ops, SparseCore 0:
  10.7 75.4 all-gather.12
  87.8 21.0 all-gather.6
  111.1 51.5 all-gather.8
  164.1 115.7 all-gather.14
  281.9 49.0 all-gather.10
